TPU v7x, 512 devices: a whole 4x4x16 slice. The times are simulated.
512 devices in a mesh: dp: 32 (over y_hi, z), expert: 16 (over y_lo, x, core).
Axes of the slice: x: 4, y: 4 (y_hi: 2, y_lo: 2; y = y_hi * 2 + y_lo), z: 16, core: 2. Of those that a mesh axis runs over, the one named last changes fastest.
Arguments:
- residual_in: bfloat16 [1536, 2048], P('dp', 'expert'), may hold values from -36 to 36
- attention_values: bfloat16 [1536, 2048], P('dp', 'expert'), may hold values from -6 to 6
- out_weight: bfloat16 [2048, 2048], P('expert', 'dp'), may hold values from -0.25 to 0.25
- norm_gain: float32 [2048], replicated, may hold values from 0.1 to 1.9
- shared_gate: bfloat16 [2816, 2048], P('expert'), may hold values from -0.125 to 0.125
- shared_up: bfloat16 [2816, 2048], P('expert'), may hold values from -0.125 to 0.125
- shared_down: bfloat16 [2816, 2048], P('expert'), may hold values from -0.15625 to 0.15625
- expert_gate: bfloat16 [64, 1408, 2048], P('dp', 'expert'), may hold values from -0.125 to 0.125
- expert_up: bfloat16 [64, 1408, 2048], P('dp', 'expert'), may hold values from -0.125 to 0.125
- expert_down: bfloat16 [64, 1408, 2048], P('dp', 'expert'), may hold values from -0.21875 to 0.21875
- expert_ids: int32 [1536, 6], P('dp'), may hold values from 0 to 63, all different within a row; in each aligned block of 48 rows (0 to 47, 48 to 95, ...) at most 10 rows name the same one
- gate_weights: float32 [1536, 6], P('dp'), may hold values from 0.02 to 0.5
Outputs:
- layer_out: bfloat16 [1536, 2048], P('dp', 'expert')
Inputs may be any that keep to these rules, and one draw needn't show every extreme that they name: `expert_ids`: each token names 6 different experts; among the 48 tokens of one index of dp (aligned blocks of rows) no expert is named by more than 10 tokens, a bound that some block reaches.
All inputs are finite; a program needn't handle non-finite values.
Results may differ from a plain program's by a relative error of at most 0.0035.
Values may be sent and summed in bfloat16 or wider, within the bound.
A program may use at most 128 MiB of HBM per device.

v0:
```python
import jax
import jax.numpy as jnp
from jax import lax
from jax.sharding import PartitionSpec as P

epsilon = 1e-06


def by_rows(left, right):
    return lax.dot_general(
        left, right, (((1,), (1,)), ((), ())), preferred_element_type=jnp.float32
    )


def expert_slots(expert_ids, experts, capacity):
    token_count, choose = expert_ids.shape
    flat_ids = expert_ids.reshape(-1)
    matches = (flat_ids[:, None] == jnp.arange(experts, dtype=jnp.int32)[None, :]).astype(jnp.int32)
    earlier = jnp.cumsum(matches, axis=0) - matches
    target = flat_ids * capacity + jnp.sum(earlier * matches, axis=1)
    return target.reshape(token_count, choose)


def collect_rows(returned_rows, slot_index, gate_weights):
    token_count, choose = slot_index.shape
    picked = returned_rows[slot_index.reshape(-1)].reshape(
        token_count, choose, returned_rows.shape[1]
    )
    return jnp.sum(picked * gate_weights[:, :, None], axis=1)


def expert_apply(buffer, expert_gate, expert_up, expert_down):
    gate_part = jnp.einsum(
        "slmd,lfd->slmf", buffer, expert_gate, preferred_element_type=jnp.float32
    )
    up_part = jnp.einsum("slmd,lfd->slmf", buffer, expert_up, preferred_element_type=jnp.float32)
    active = (jax.nn.silu(gate_part) * up_part).astype(jnp.bfloat16)
    return jnp.einsum("slmf,lfd->slmd", active, expert_down, preferred_element_type=jnp.float32)


def shards(
    residual_in,
    attention_values,
    out_weight,
    norm_gain,
    shared_gate,
    shared_up,
    shared_down,
    expert_gate,
    expert_up,
    expert_down,
    expert_ids,
    gate_weights,
):
    row_count = residual_in.shape[0]
    slice_width = residual_in.shape[1]
    expert_size = lax.axis_size("expert")
    batch_size = lax.axis_size("dp")
    full_width = slice_width * expert_size
    local_experts = expert_gate.shape[0]
    experts = local_experts * batch_size
    choose = expert_ids.shape[1]
    capacity = 2 * ((row_count * choose + experts - 1) // experts)
    column_start = lax.axis_index("expert") * slice_width
    head_terms = jnp.dot(
        attention_values,
        lax.all_gather(out_weight, "dp", axis=1, tiled=True),
        preferred_element_type=jnp.float32,
    )
    residual_own = residual_in.astype(jnp.float32)
    current = lax.dynamic_slice_in_dim(head_terms, column_start, slice_width, 1)
    head_terms = lax.dynamic_update_slice_in_dim(
        head_terms, current + residual_own, column_start, 1
    )
    residual = lax.psum(head_terms, "expert")
    inverse_rms = lax.rsqrt(jnp.mean(residual * residual, axis=1, keepdims=True) + epsilon)
    normed = (residual * inverse_rms * norm_gain).astype(jnp.bfloat16)
    residual_slice = lax.dynamic_slice_in_dim(residual, column_start, slice_width, 1)
    shared_active = (jax.nn.silu(by_rows(normed, shared_gate)) * by_rows(normed, shared_up)).astype(
        jnp.bfloat16
    )
    shared_terms = jnp.dot(shared_active, shared_down, preferred_element_type=jnp.float32)
    slot_index = expert_slots(expert_ids, experts, capacity)
    places = (
        slot_index[:, :, None] == jnp.arange(experts * capacity, dtype=jnp.int32)[None, None, :]
    )
    selector = jnp.any(places, axis=1).astype(jnp.bfloat16)
    slot_rows = lax.dot_general(
        selector, normed, (((0,), (0,)), ((), ())), preferred_element_type=jnp.float32
    )
    buffer = slot_rows.astype(jnp.bfloat16).reshape(batch_size, local_experts, capacity, full_width)
    partials = expert_apply(
        lax.all_to_all(buffer, "dp", split_axis=0, concat_axis=0, tiled=True),
        expert_gate,
        expert_up,
        expert_down,
    )
    returned = lax.all_to_all(partials, "dp", split_axis=0, concat_axis=0, tiled=True)
    routed_terms = collect_rows(
        returned.reshape(experts * capacity, full_width), slot_index, gate_weights
    )
    totals = lax.psum_scatter(
        shared_terms + routed_terms, "expert", scatter_dimension=1, tiled=True
    )
    return (residual_slice + totals).astype(jnp.bfloat16)


def solution(mesh):
    return jax.shard_map(
        shards,
        mesh=mesh,
        in_specs=(
            P("dp", "expert"),
            P("dp", "expert"),
            P("expert", "dp"),
            P(),
            P("expert", None),
            P("expert", None),
            P("expert", None),
            P("dp", "expert", None),
            P("dp", "expert", None),
            P("dp", "expert", None),
            P("dp", None),
            P("dp", None),
        ),
        out_specs=P("dp", "expert"),
        check_vma=False,
    )
```

profile of v0, /device:TPU:32, one launch (start us, length us, event | category | flops | bytes accessed | tf_op | source)
XLA Modules:
  0.0 723.8 jit_solution(14739102939381321039)
XLA Ops:
  6.5 81.4 %all_gather.3 = bf16[128,2048]{0,1:T(8,128)(2,1)S(1)} all-gather(bf16[128,64]{0,1:T(8,128)(2,1)} %param.14), channel_id=1, replica_groups=mesh['dp'=32,'expert'=16] {'dp'}, dimensions={1}, use_global_device_ids=true | all-gather | bytes 540672 | tf_op jit(solution)/shard_map/all_gather | solution.py:67
  87.9 1.0 fusion.42
  88.9 0.7 add_dynamic-update-slice_fusion
  89.6 0.7 copy-done.1
  90.4 0.8 copy.41
  91.2 0.1 eq.35
  91.4 0.9 reduce-window.6
  92.3 0.2 slice_reduce_fusion
  92.8 0.6 broadcast_multiply_fusion
  93.5 0.8 fusion.19
  94.3 121.7 %all-reduce.3.cloned.1.call-done = f32[48,2048]{1,0:T(8,128)} async-done(((f32[48,2048]{1,0:T(8,128)}), f32[48,2048]{1,0:T(8,128)}) %all-reduce.3.cloned.1.call-update) | async-done | bytes 393232 | tf_op jit(solution)/shard_map/psum | solution.py:75
  216.0 1.1 multiply_reduce_fusion.1
  217.1 1.1 multiply_convert_fusion
  218.3 1.6 convolution_convert_fusion
  219.9 2.8 reshape.68
  222.7 4.9 copy.46
  227.6 138.5 %all_to_all.10 = bf16[32,2,10,2048]{3,1,2,0:T(2,128)(2,1)S(1)} all-to-all(bf16[32,2,10,2048]{3,1,2,0:T(2,128)(2,1)S(1)} %copy.46), channel_id=1, replica_groups=mesh['dp'=32,'expert'=16] {'dp'}, dimensions={0} | all-to-all | bytes 5242880 | tf_op jit(solution)/shard_map/all_to_all | solution.py:93
  366.1 2.3 fusion.4
  368.4 5.9 convolution_bitcast_fusion
  374.3 8.8 %copy.49 = f32[32,2,10,2048]{3,1,2,0:T(2,128)} copy(f32[32,2,10,2048]{3,0,2,1:T(8,128)} %convolution_bitcast_fusion) | data formatting | bytes 10485760 | tf_op jit(solution)/shard_map/slmf,lfd->slmd/transpose | solution.py:38
  383.1 4.8 all-to-all-start.1
  387.9 0.3 reduce-scatter.2.cloned.1.call-start
  388.5 0.3 fusion.43
  388.8 234.1 %all-to-all-done.1 = f32[32,2,10,2048]{3,1,2,0:T(2,128)} async-done(((f32[32,2,10,2048]{3,1,2,0:T(2,128)}), f32[32,2,10,2048]{3,1,2,0:T(2,128)}, u32[]{:S(2)}, u32[]{:S(2)}) %all-to-all-start.1) | async-done | bytes 5242912 | tf_op jit(solution)/shard_map/all_to_all | solution.py:98
  623.0 10.3 %copy.50 = f32[32,2,10,2048]{3,2,1,0:T(8,128)} copy(f32[32,2,10,2048]{3,1,2,0:T(2,128)} %all-to-all-done.1) | data formatting | bytes 10485760 | tf_op jit(solution)/shard_map/all_to_all | solution.py:98
  633.3 7.4 %reshape.69 = f32[640,2048]{1,0:T(8,128)} reshape(f32[32,2,10,2048]{3,2,1,0:T(8,128)} %copy.50) | data formatting | bytes 10485760 | tf_op jit(solution)/shard_map/reshape | solution.py:100
  640.7 6.8 gather_fusion
  647.4 1.8 reshape.70
  649.3 3.1 multiply_reduce_fusion
  652.5 1.4 convolution_add_fusion
  653.9 61.7 %reduce-scatter.2.cloned.1.call-done = f32[48,128]{1,0:T(8,128)} async-done(((f32[48,2048]{1,0:T(8,128)}), f32[48,128]{1,0:T(8,128)}) %reduce-scatter.2.cloned.1.call-update) | async-done | bytes 24592 | tf_op jit(solution)/shard_map/reduce_scatter | solution.py:102
  715.6 1.4 add_convert_fusion
  (32 shorter events, 0.7 us)
Async XLA Ops:
  6.5 361.9 %copy-start = (bf16[2,88,2048]{2,1,0:T(8,128)(2,1)S(1)}, bf16[2,88,2048]{2,1,0:T(8,128)(2,1)}, u32[]{:S(2)}) copy-start(bf16[2,88,2048]{2,1,0:T(8,128)(2,1)} %param.21) | copy-start | bytes 2162692
  6.5 210.6 %copy-start.6 = (f32[2048]{0:T(1024)S(1)}, f32[2048]{0:T(1024)}, u32[]{:S(2)}) copy-start(f32[2048]{0:T(1024)} %param.15) | copy-start | bytes 24580
  6.5 209.5 %all-reduce.3.cloned.1.call-start = ((), (), s32[]{:S(2)}) async-start(), calls=%async_computation.3 | async-start | bytes 786432 | tf_op jit(solution)/shard_map/psum | solution.py:75
  89.6 0.7 copy-start.1
  227.6 138.5 %copy-start.8 = (bf16[2,88,2048]{2,1,0:T(8,128)(2,1)S(1)}, bf16[2,88,2048]{2,1,0:T(8,128)(2,1)}, u32[]{:S(2)}) copy-start(bf16[2,88,2048]{2,1,0:T(8,128)(2,1)} %param.19) | copy-start | bytes 2162692
  383.1 5.1 copy-start.5
  383.1 5.2 copy-start.7
  383.1 5.4 copy-start.4
  383.1 239.9 %all-to-all-start.1 = ((f32[32,2,10,2048]{3,1,2,0:T(2,128)}), f32[32,2,10,2048]{3,1,2,0:T(2,128)}, u32[]{:S(2)}, u32[]{:S(2)}) async-start(f32[32,2,10,2048]{3,1,2,0:T(2,128)} %copy.49), calls=%async_computation.1 | async-start | bytes 10485760 | tf_op jit(solution)/shard_map/all_to_all | solution.py:98
  387.9 327.7 %reduce-scatter.2.cloned.1.call-start = ((), (), s32[]{:S(2)}) async-start(), calls=%async_computation.4 | async-start | bytes 417792 | tf_op jit(solution)/shard_map/reduce_scatter | solution.py:102
  649.3 3.1 copy-start.2
  649.3 3.2 copy-start.3
Sparse Core Ops, SparseCore 0:
  90.5 125.4 all-reduce.2
  654.0 61.5 reduce-scatter.1
where the time goes:
time: 725 us; the launch traced here: 724 us
  waiting for transfers between devices  418 us (58%)
  blocking collectives  220 us (30%)
  local copies, waits for them, and re-layouts  45.1 us (6%)
  between operations  13.6 us (2%)
  matrix products  12.6 us (2%)
  other arithmetic  9.98 us (1%)
    all_to_all x1, waiting for transfers between devices, shards(): lax.all_to_all(partials, 'dp', split_axis=0, concat_axis=0, tiled=True)  234 us
    all_to_all x1, blocking collectives, shards(): lax.all_to_all(buffer, 'dp', split_axis=0, concat_axis=0, tiled=True)  138 us
    psum x1, waiting for transfers between devices, shards(): residual = lax.psum(head_terms, 'expert')  122 us
    all_gather x1, blocking collectives, shards(): lax.all_gather(out_weight, 'dp', axis=1, tiled=True)  81.4 us
    reduce_scatter x1, waiting for transfers between devices, shards(): lax.psum_scatter(shared_terms + routed_terms, 'expert', scatter_dimension...  61.7 us
  transfers between devices with their start and end apart: 3, of which 3 were waited for; matrix products, arithmetic and copies ran while one was open for 1% of the time, Pallas kernels for 0%

commit v1 on v0

--- a/solution.py
+++ b/solution.py
@@ -64,7 +64,9 @@
     column_start = lax.axis_index("expert") * slice_width
     head_terms = jnp.dot(
         attention_values,
-        lax.all_gather(out_weight, "dp", axis=1, tiled=True),
+        jnp.concatenate(
+            lax.all_to_all(jnp.stack([out_weight] * lax.axis_size("dp")), "dp", 0, 0), axis=1
+        ),
         preferred_element_type=jnp.float32,
     )
     residual_own = residual_in.astype(jnp.float32)

time: 725 us -> 693 us (0.956)
  blocking collectives: 220 us -> 138 us
  waiting for transfers between devices: 418 us -> 449 us
  starting transfers between devices: 5.08 us -> 23.1 us
    all_gather x1 -> x0, blocking collectives: 81.4 us -> none  [shards(): lax.all_gather(out_weight, 'dp', axis=1, tiled=True)]
    all_to_all x0 -> x1, waiting for transfers between devices: none -> 31.5 us  [shards(): lax.all_to_all(jnp.stack([out_weight] * lax.axis_size('dp')), 'dp', 0, 0)]
    all_to_all x0 -> x1, starting transfers between devices: none -> 18 us  [shards(): lax.all_to_all(jnp.stack([out_weight] * lax.axis_size('dp')), 'dp', 0, 0)]
  transfers between devices with their start and end apart: 3 -> 4, of which waited for: 3 -> 4; matrix products, arithmetic and copies ran while one was open for 1% -> 1% of each run, Pallas kernels for 0% -> 0%
where the time goes in v1:
time: 693 us
  waiting for transfers between devices  449 us (65%)
  blocking collectives  138 us (20%)
  local copies, waits for them, and re-layouts  46.8 us (7%)
  starting transfers between devices  23.1 us (3%)
  between operations  13.6 us (2%)
  matrix products  12.6 us (2%)
  other arithmetic  9.28 us (1%)
    all_to_all x1, waiting for transfers between devices, shards(): lax.all_to_all(partials, 'dp', split_axis=0, concat_axis=0, tiled=True)  234 us
    all_to_all x1, blocking collectives, shards(): lax.all_to_all(buffer, 'dp', split_axis=0, concat_axis=0, tiled=True)  138 us
    psum x1, waiting for transfers between devices, shards(): residual = lax.psum(head_terms, 'expert')  121 us
    reduce_scatter x1, waiting for transfers between devices, shards(): lax.psum_scatter(shared_terms + routed_terms, 'expert', scatter_dimension...  61.7 us
    all_to_all x1, waiting for transfers between devices, shards(): lax.all_to_all(jnp.stack([out_weight] * lax.axis_size('dp')), 'dp', 0, 0)  31.5 us
    all_to_all x1, starting transfers between devices, shards(): lax.all_to_all(jnp.stack([out_weight] * lax.axis_size('dp')), 'dp', 0, 0)  18 us
  transfers between devices with their start and end apart: 4, of which 4 were waited for; matrix products, arithmetic and copies ran while one was open for 1% of the time, Pallas kernels for 0%

profile of v1, /device:TPU:32, one launch (start us, length us, event | category | flops | bytes accessed | tf_op | source)
XLA Modules:
  0.0 692.6 jit_solution(11471674108439746547)
XLA Ops:
  6.5 1.7 stack.2
  8.2 18.0 %all-to-all-start = ((bf16[32,128,64]{1,2,0:T(8,128)(2,1)}), bf16[32,128,64]{1,2,0:T(8,128)(2,1)S(1)}, u32[]{:S(2)}, u32[]{:S(2)}) async-start(bf16[32,128,64]{1,2,0:T(8,128)(2,1)} %stack.2), calls=%async_computation | async-start | bytes 1048576 | tf_op jit(solution)/shard_map/all_to_all | solution.py:68
  26.3 0.8 copy.42
  27.2 0.9 reduce-window.6
  28.1 0.2 slice_reduce_fusion
  28.5 31.5 %all-to-all-done = bf16[32,128,64]{1,2,0:T(8,128)(2,1)S(1)} async-done(((bf16[32,128,64]{1,2,0:T(8,128)(2,1)}), bf16[32,128,64]{1,2,0:T(8,128)(2,1)S(1)}, u32[]{:S(2)}, u32[]{:S(2)}) %all-to-all-start) | async-done | bytes 524320 | tf_op jit(solution)/shard_map/all_to_all | solution.py:68
  60.0 1.0 fusion.42
  61.0 0.7 copy-done.1
  61.9 0.6 broadcast_multiply_fusion
  62.6 0.8 fusion.19
  63.4 121.4 %all-reduce.3.cloned.1.call-done = f32[48,2048]{1,0:T(8,128)} async-done(((f32[48,2048]{1,0:T(8,128)}), f32[48,2048]{1,0:T(8,128)}) %all-reduce.3.cloned.1.call-update) | async-done | bytes 393232 | tf_op jit(solution)/shard_map/psum | solution.py:77
  184.7 1.1 multiply_reduce_fusion.1
  185.9 1.1 multiply_convert_fusion
  187.0 1.6 convolution_convert_fusion
  188.6 2.8 reshape.78
  191.4 4.9 copy.47
  196.4 138.5 %all_to_all.15 = bf16[32,2,10,2048]{3,1,2,0:T(2,128)(2,1)S(1)} all-to-all(bf16[32,2,10,2048]{3,1,2,0:T(2,128)(2,1)S(1)} %copy.47), channel_id=1, replica_groups=mesh['dp'=32,'expert'=16] {'dp'}, dimensions={0} | all-to-all | bytes 5242880 | tf_op jit(solution)/shard_map/all_to_all | solution.py:95
  334.8 2.3 fusion.4
  337.1 5.9 convolution_bitcast_fusion
  343.0 8.8 %copy.50 = f32[32,2,10,2048]{3,1,2,0:T(2,128)} copy(f32[32,2,10,2048]{3,0,2,1:T(8,128)} %convolution_bitcast_fusion) | data formatting | bytes 10485760 | tf_op jit(solution)/shard_map/slmf,lfd->slmd/transpose | solution.py:38
  351.9 4.8 all-to-all-start.2
  356.7 0.3 reduce-scatter.2.cloned.1.call-start
  357.3 0.3 fusion.43
  357.6 234.1 %all-to-all-done.2 = f32[32,2,10,2048]{3,1,2,0:T(2,128)} async-done(((f32[32,2,10,2048]{3,1,2,0:T(2,128)}), f32[32,2,10,2048]{3,1,2,0:T(2,128)}, u32[]{:S(2)}, u32[]{:S(2)}) %all-to-all-start.2) | async-done | bytes 5242912 | tf_op jit(solution)/shard_map/all_to_all | solution.py:100
  591.7 10.3 %copy.51 = f32[32,2,10,2048]{3,2,1,0:T(8,128)} copy(f32[32,2,10,2048]{3,1,2,0:T(2,128)} %all-to-all-done.2) | data formatting | bytes 10485760 | tf_op jit(solution)/shard_map/all_to_all | solution.py:100
  602.0 7.4 %reshape.79 = f32[640,2048]{1,0:T(8,128)} reshape(f32[32,2,10,2048]{3,2,1,0:T(8,128)} %copy.51) | data formatting | bytes 10485760 | tf_op jit(solution)/shard_map/reshape | solution.py:102
  609.4 6.8 gather_fusion
  616.2 1.8 reshape.80
  618.0 3.1 multiply_reduce_fusion
  621.2 1.4 convolution_add_fusion
  622.7 61.7 %reduce-scatter.2.cloned.1.call-done = f32[48,128]{1,0:T(8,128)} async-done(((f32[48,2048]{1,0:T(8,128)}), f32[48,128]{1,0:T(8,128)}) %reduce-scatter.2.cloned.1.call-update) | async-done | bytes 24592 | tf_op jit(solution)/shard_map/reduce_scatter | solution.py:104
  684.4 1.4 add_convert_fusion
  (36 shorter events, 0.9 us)
Async XLA Ops:
  6.5 330.6 %copy-start = (bf16[2,88,2048]{2,1,0:T(8,128)(2,1)S(1)}, bf16[2,88,2048]{2,1,0:T(8,128)(2,1)}, u32[]{:S(2)}) copy-start(bf16[2,88,2048]{2,1,0:T(8,128)(2,1)} %param.21) | copy-start | bytes 2162692
  6.5 54.4 %copy-start.6 = (bf16[48,128]{1,0:T(8,128)(2,1)S(1)}, bf16[48,128]{1,0:T(8,128)(2,1)}, u32[]{:S(2)}) copy-start(bf16[48,128]{1,0:T(8,128)(2,1)} %param.12) | copy-start | bytes 36868
  6.5 179.3 %copy-start.7 = (f32[2048]{0:T(1024)S(1)}, f32[2048]{0:T(1024)}, u32[]{:S(2)}) copy-start(f32[2048]{0:T(1024)} %param.15) | copy-start | bytes 24580
  8.2 51.7 %all-to-all-start = ((bf16[32,128,64]{1,2,0:T(8,128)(2,1)}), bf16[32,128,64]{1,2,0:T(8,128)(2,1)S(1)}, u32[]{:S(2)}, u32[]{:S(2)}) async-start(bf16[32,128,64]{1,2,0:T(8,128)(2,1)} %stack.2), calls=%async_computation | async-start | bytes 1048576 | tf_op jit(solution)/shard_map/all_to_all | solution.py:68
  26.2 158.5 %all-reduce.3.cloned.1.call-start = ((), (), s32[]{:S(2)}) async-start(), calls=%async_computation.4 | async-start | bytes 786432 | tf_op jit(solution)/shard_map/psum | solution.py:77
  61.0 0.7 copy-start.1
  196.3 138.5 %copy-start.9 = (bf16[2,88,2048]{2,1,0:T(8,128)(2,1)S(1)}, bf16[2,88,2048]{2,1,0:T(8,128)(2,1)}, u32[]{:S(2)}) copy-start(bf16[2,88,2048]{2,1,0:T(8,128)(2,1)} %param.19) | copy-start | bytes 2162692
  351.9 5.1 copy-start.5
  351.9 5.3 copy-start.8
  351.9 5.4 copy-start.4
  351.9 239.9 %all-to-all-start.2 = ((f32[32,2,10,2048]{3,1,2,0:T(2,128)}), f32[32,2,10,2048]{3,1,2,0:T(2,128)}, u32[]{:S(2)}, u32[]{:S(2)}) async-start(f32[32,2,10,2048]{3,1,2,0:T(2,128)} %copy.50), calls=%async_computation.2 | async-start | bytes 10485760 | tf_op jit(solution)/shard_map/all_to_all | solution.py:100
  356.7 327.7 %reduce-scatter.2.cloned.1.call-start = ((), (), s32[]{:S(2)}) async-start(), calls=%async_computation.5 | async-start | bytes 417792 | tf_op jit(solution)/shard_map/reduce_scatter | solution.py:104
  618.0 3.1 copy-start.2
  618.0 3.2 copy-start.3
Sparse Core Ops, SparseCore 0:
  61.9 122.8 all-reduce.2
  622.8 61.5 reduce-scatter.1

commit v2 on v0

--- a/solution.py
+++ b/solution.py
@@ -72,7 +72,7 @@
     head_terms = lax.dynamic_update_slice_in_dim(
         head_terms, current + residual_own, column_start, 1
     )
-    residual = lax.psum(head_terms, "expert")
+    residual = jnp.sum(lax.all_gather(head_terms, "expert"), axis=0)
     inverse_rms = lax.rsqrt(jnp.mean(residual * residual, axis=1, keepdims=True) + epsilon)
     normed = (residual * inverse_rms * norm_gain).astype(jnp.bfloat16)
     residual_slice = lax.dynamic_slice_in_dim(residual, column_start, slice_width, 1)

time: 725 us -> 642 us (0.89)
  waiting for transfers between devices: 418 us -> 333 us
    psum x1 -> x0, waiting for transfers between devices: 122 us -> none  [shards(): residual = lax.psum(head_terms, 'expert')]
    all_gather x0 -> x1, waiting for transfers between devices: none -> 39.9 us  [shards(): residual = jnp.sum(lax.all_gather(head_terms, 'expert'), axis=0)]
where the time goes in v2:
time: 642 us; the launch traced here: 641 us
  waiting for transfers between devices  333 us (52%)
  blocking collectives  220 us (34%)
  local copies, waits for them, and re-layouts  45.1 us (7%)
  between operations  13.6 us (2%)
  matrix products  12.6 us (2%)
  other arithmetic  11.1 us (2%)
    all_to_all x1, waiting for transfers between devices, shards(): lax.all_to_all(partials, 'dp', split_axis=0, concat_axis=0, tiled=True)  234 us
    all_to_all x1, blocking collectives, shards(): lax.all_to_all(buffer, 'dp', split_axis=0, concat_axis=0, tiled=True)  139 us
    all_gather x1, blocking collectives, shards(): lax.all_gather(out_weight, 'dp', axis=1, tiled=True)  81.4 us
    reduce_scatter x1, waiting for transfers between devices, shards(): lax.psum_scatter(shared_terms + routed_terms, 'expert', scatter_dimension...  59.4 us
    all_gather x1, waiting for transfers between devices, shards(): residual = jnp.sum(lax.all_gather(head_terms, 'expert'), axis=0)  39.9 us
  transfers between devices with their start and end apart: 3, of which 3 were waited for; matrix products, arithmetic and copies ran while one was open for 1% of the time, Pallas kernels for 0%

profile of v2, /device:TPU:32, one launch (start us, length us, event | category | flops | bytes accessed | tf_op | source)
XLA Modules:
  0.0 641.1 jit_solution(18441331510742704819)
XLA Ops:
  6.5 81.4 %all_gather.11 = bf16[128,2048]{0,1:T(8,128)(2,1)S(1)} all-gather(bf16[128,64]{0,1:T(8,128)(2,1)} %param.14), channel_id=1, replica_groups=mesh['dp'=32,'expert'=16] {'dp'}, dimensions={1}, use_global_device_ids=true | all-gather | bytes 540672 | tf_op jit(solution)/shard_map/all_gather | solution.py:67
  87.9 1.0 fusion.42
  89.0 0.7 bitcast_dynamic-update-slice_fusion
  89.7 0.8 copy-done.2
  90.6 0.1 eq.35
  90.8 0.9 reduce-window.6
  91.7 0.2 slice_reduce_fusion
  92.2 0.6 broadcast_multiply_fusion
  92.9 0.8 fusion.19
  93.7 39.9 %all-gather.2.cloned.1.call-done = f32[16,48,2048]{2,1,0:T(8,128)} async-done(((f32[1,48,2048]{2,1,0:T(8,128)}), f32[16,48,2048]{2,1,0:T(8,128)}) %all-gather.2.cloned.1.call-update) | async-done | bytes 6291472 | tf_op jit(solution)/shard_map/all_gather | solution.py:75
  133.6 3.1 reduce_sum.40
  136.8 0.1 multiply_reduce_fusion.1
  136.9 0.6 copy-done.1
  137.6 1.6 convolution_convert_fusion
  139.3 2.8 reshape.70
  142.0 4.9 copy.46
  147.0 139.1 %all_to_all.10 = bf16[32,2,10,2048]{3,1,2,0:T(2,128)(2,1)S(1)} all-to-all(bf16[32,2,10,2048]{3,1,2,0:T(2,128)(2,1)S(1)} %copy.46), channel_id=1, replica_groups=mesh['dp'=32,'expert'=16] {'dp'}, dimensions={0} | all-to-all | bytes 5242880 | tf_op jit(solution)/shard_map/all_to_all | solution.py:93
  286.1 2.3 fusion.4
  288.4 5.9 convolution_bitcast_fusion
  294.3 8.8 %copy.49 = f32[32,2,10,2048]{3,1,2,0:T(2,128)} copy(f32[32,2,10,2048]{3,0,2,1:T(8,128)} %convolution_bitcast_fusion) | data formatting | bytes 10485760 | tf_op jit(solution)/shard_map/slmf,lfd->slmd/transpose | solution.py:38
  303.1 4.8 all-to-all-start.1
  307.9 0.3 reduce-scatter.2.cloned.1.call-start
  308.5 0.3 fusion.43
  308.8 233.7 %all-to-all-done.1 = f32[32,2,10,2048]{3,1,2,0:T(2,128)} async-done(((f32[32,2,10,2048]{3,1,2,0:T(2,128)}), f32[32,2,10,2048]{3,1,2,0:T(2,128)}, u32[]{:S(2)}, u32[]{:S(2)}) %all-to-all-start.1) | async-done | bytes 5242912 | tf_op jit(solution)/shard_map/all_to_all | solution.py:98
  542.6 10.3 %copy.50 = f32[32,2,10,2048]{3,2,1,0:T(8,128)} copy(f32[32,2,10,2048]{3,1,2,0:T(2,128)} %all-to-all-done.1) | data formatting | bytes 10485760 | tf_op jit(solution)/shard_map/all_to_all | solution.py:98
  552.9 7.4 %reshape.71 = f32[640,2048]{1,0:T(8,128)} reshape(f32[32,2,10,2048]{3,2,1,0:T(8,128)} %copy.50) | data formatting | bytes 10485760 | tf_op jit(solution)/shard_map/reshape | solution.py:100
  560.3 6.8 %gather_fusion = f32[288,2048]{1,0:T(8,128)S(1)} fusion(f32[640,2048]{1,0:T(8,128)} %reshape.71, s32[1024]{0:T(1024)S(1)} %pad_clamp_fusion), kind=kCustom, calls=%fused_computation | custom fusion | bytes 4719744 | tf_op jit(solution)/shard_map/gather | solution.py:26
  567.1 1.8 reshape.72
  568.9 3.1 multiply_reduce_fusion
  572.1 1.4 convolution_add_fusion
  573.5 59.4 %reduce-scatter.2.cloned.1.call-done = f32[48,128]{1,0:T(8,128)} async-done(((f32[48,2048]{1,0:T(8,128)}), f32[48,128]{1,0:T(8,128)}) %reduce-scatter.2.cloned.1.call-update) | async-done | bytes 24592 | tf_op jit(solution)/shard_map/reduce_scatter | solution.py:102
  632.9 1.4 add_convert_fusion
  (38 shorter events, 0.9 us)
Async XLA Ops:
  6.5 281.9 %copy-start = (bf16[2,88,2048]{2,1,0:T(8,128)(2,1)S(1)}, bf16[2,88,2048]{2,1,0:T(8,128)(2,1)}, u32[]{:S(2)}) copy-start(bf16[2,88,2048]{2,1,0:T(8,128)(2,1)} %param.21) | copy-start | bytes 2162692
  6.5 83.9 %copy-start.8 = (s32[48,6]{0,1:T(8,128)S(1)}, s32[48,6]{0,1:T(8,128)}, u32[]{:S(2)}) copy-start(s32[48,6]{0,1:T(8,128)} %param.22) | copy-start | bytes 3460
  6.5 127.1 %all-gather.2.cloned.1.call-start = ((), (), s32[]{:S(2)}) async-start(), calls=%async_computation.3 | async-start | bytes 6684672 | tf_op jit(solution)/shard_map/all_gather | solution.py:75
  89.7 0.8 copy-start.2
  93.7 43.8 %copy-start.7 = (f32[2048]{0:T(1024)S(1)}, f32[2048]{0:T(1024)}, u32[]{:S(2)}) copy-start(f32[2048]{0:T(1024)} %param.15) | copy-start | bytes 24580
  136.8 0.7 copy-start.1
  147.0 139.1 %copy-start.10 = (bf16[2,88,2048]{2,1,0:T(8,128)(2,1)S(1)}, bf16[2,88,2048]{2,1,0:T(8,128)(2,1)}, u32[]{:S(2)}) copy-start(bf16[2,88,2048]{2,1,0:T(8,128)(2,1)} %param.19) | copy-start | bytes 2162692
  303.1 5.1 copy-start.6
  303.1 5.2 copy-start.9
  303.1 5.4 copy-start.5
  303.1 239.5 %all-to-all-start.1 = ((f32[32,2,10,2048]{3,1,2,0:T(2,128)}), f32[32,2,10,2048]{3,1,2,0:T(2,128)}, u32[]{:S(2)}, u32[]{:S(2)}) async-start(f32[32,2,10,2048]{3,1,2,0:T(2,128)} %copy.49), calls=%async_computation.1 | async-start | bytes 10485760 | tf_op jit(solution)/shard_map/all_to_all | solution.py:98
  307.9 325.0 %reduce-scatter.2.cloned.1.call-start = ((), (), s32[]{:S(2)}) async-start(), calls=%async_computation.4 | async-start | bytes 417792 | tf_op jit(solution)/shard_map/reduce_scatter | solution.py:102
  568.9 3.1 copy-start.3
  568.9 3.2 copy-start.4
Sparse Core Ops, SparseCore 0:
  90.6 42.9 all-gather.1
  573.6 59.2 reduce-scatter.1
